TPU v7x, 32 devices: a whole 2x2x4 slice. The times are simulated.
32 devices in a mesh: dp: 8 (over z, y), mp: 4 (over x, core).
Axes of the slice: x: 2, y: 2, z: 4, core: 2. Of those that a mesh axis runs over, the one named last changes fastest.
Arguments:
- hidden: bfloat16 [8192, 5120], P('dp'), may hold values from -6 to 6
- exit_depth: int32 [8192], P('dp'), may hold values from 0 to 3, as said below
- seq_ids: int32 [8192], P('dp'), may hold values from 0 to 3, as said below
- dest: int32 [8192], P('dp'), may hold values from 0 to 7, as said below
- norm_gain: bfloat16 [5120], replicated, may hold values from 0.5 to 1.5
- w_query: bfloat16 [5120, 3072], P(None, 'mp'), may hold values from -4 to 4
- w_key: bfloat16 [5120, 3072], P(None, 'mp'), may hold values from -4 to 4
- w_value: bfloat16 [5120, 3072], P(None, 'mp'), may hold values from -0.078125 to 0.078125
- w_out: bfloat16 [3072, 5120], P('mp'), may hold values from -0.4375 to 0.4375
Outputs:
- next_rows: bfloat16 [6144, 5120], P('dp', 'mp')
Inputs may be any that keep to these rules, and one draw needn't show every extreme that they name: exit_depth is 3 for at most 768 tokens of one sequence, and for exactly that many in some sequence. seq_ids never fall along a sequence. `dest`: within one sequence, at most 96 tokens with exit depth 3 name the same destination, and some sequence has exactly 96 that do.
All inputs are finite; a program needn't handle non-finite values.
Results may differ from a plain program's by a relative error of at most 0.014.
Values may be sent and summed in bfloat16 or wider, within the bound.
A program may use at most 128 MiB of HBM per device.

v0:
```python
import functools
import math

import jax
import jax.numpy as jnp
import numpy as np
from jax import lax
from jax.experimental import pallas as pl
from jax.experimental.pallas import tpu as pltpu
from jax.sharding import PartitionSpec as P

HD = 128
CHUNKS = 8
LAG = 1
ANY = pl.ANY
VMEM = pltpu.VMEM


def rope_tables(tokens):
    half = HD // 2
    frequency = 10000.0 ** (-np.arange(half, dtype=np.float64) / half)
    angle = np.arange(tokens, dtype=np.float64)[:, None] * frequency[None, :]
    cosine, sine = np.cos(angle), np.sin(angle)
    return (
        np.concatenate([cosine, cosine], axis=1).astype(np.float32),
        np.concatenate([-sine, sine], axis=1).astype(np.float32),
    )


def qkv_kernel(
    blocks, bn, rows, hidden, gain, wq, wk, wv, cosine, sine, out, held, normed, wbuf, hsem, wsem
):
    step = pl.program_id(0)
    slot = lax.rem(step, 2)
    chunks = hidden.shape[0] // rows

    def fetch(index, do):
        for which, w in enumerate((wq, wk, wv)):

            @pl.when(index // blocks == which)
            def _():
                column = pl.multiple_of(lax.rem(index, blocks) * bn, bn)
                to = lax.rem(index, 2)
                do(pltpu.make_async_copy(w.at[:, pl.ds(column, bn)], wbuf.at[to], wsem.at[to]))

    def hidden_copy(r):
        part = pl.ds(r * rows, rows)
        return pltpu.make_async_copy(hidden.at[part], held.at[part], hsem.at[r])

    @pl.when(step == 0)
    def _():
        for r in range(chunks):
            hidden_copy(r).start()
        fetch(0, lambda c: c.start())

    @pl.when(step + 1 < 3 * blocks)
    def _():
        fetch(step + 1, lambda c: c.start())

    @pl.when(step == 0)
    def _():
        def normalize(r, carry):
            hidden_copy(r).wait()
            part = pl.ds(pl.multiple_of(r * rows, rows), rows)
            x = held[part, :].astype(jnp.float32)
            mean_square = jnp.mean(x * x, axis=-1, keepdims=True)
            y = x * lax.rsqrt(mean_square + 1e-05) * gain[...].astype(jnp.float32)[None, :]
            normed[part, :] = y.astype(jnp.bfloat16)
            return carry

        lax.fori_loop(0, chunks, normalize, 0)

    fetch(step, lambda c: c.wait())
    big = 2 * rows

    def product(r, rotate):
        part = pl.ds(pl.multiple_of(r * big, big), big)
        y = jnp.dot(normed[part, :], wbuf[slot], preferred_element_type=jnp.float32)
        for h in range(bn // HD):
            lanes = slice(h * HD, (h + 1) * HD)
            z = y[:, lanes]
            if rotate:
                z = z * cosine[part, :] + pltpu.roll(z, HD // 2, 1) * sine[part, :]
            out[0, part, lanes] = z.astype(jnp.bfloat16)

    for rotate in (True, False):

        @pl.when((step < 2 * blocks) == rotate)
        def _():
            def go(r, carry):
                product(r, rotate)
                return carry

            lax.fori_loop(0, hidden.shape[0] // big, go, 0)


def project(hidden, gain, wq, wk, wv):
    tokens, width = hidden.shape
    hw = wq.shape[1]
    bn = 256 if hw % 256 == 0 else HD
    blocks = hw // bn
    rows = 128
    cosine, sine = rope_tables(tokens)
    whole = lambda *shape: pl.BlockSpec(shape, lambda i: (0,) * len(shape), pipeline_mode=pl.Buffered(1))
    return pl.pallas_call(
        functools.partial(qkv_kernel, blocks, bn, rows),
        grid=(3 * blocks,),
        out_shape=jax.ShapeDtypeStruct((3, tokens, hw), jnp.bfloat16),
        in_specs=[
            pl.BlockSpec(memory_space=ANY),
            whole(width),
            pl.BlockSpec(memory_space=ANY),
            pl.BlockSpec(memory_space=ANY),
            pl.BlockSpec(memory_space=ANY),
            whole(tokens, HD),
            whole(tokens, HD),
        ],
        out_specs=pl.BlockSpec((1, tokens, bn), lambda i: (i // blocks, 0, lax.rem(i, blocks))),
        scratch_shapes=[
            VMEM((tokens, width), jnp.bfloat16),
            VMEM((tokens, width), jnp.bfloat16),
            VMEM((2, width, bn), jnp.bfloat16),
            pltpu.SemaphoreType.DMA((tokens // rows,)),
            pltpu.SemaphoreType.DMA((2,)),
        ],
        compiler_params=pltpu.CompilerParams(vmem_limit_bytes=60 * 2**20),
        name="qkv",
    )(hidden, gain, wq, wk, wv, cosine, sine)


def tail_kernel(
    peers, groups, per_chunk, qkv, meta_row, hidden, w_out, out,
    wbuf, residual, slot_row, pair_send, pair_own, pair_recv, x_send, x_recv, acc, updated,
    wsem, rsem, pair_ssem, pair_rsem, x_ssem, x_rsem, row_ssem, row_rsem, own_sem,
):
    chunks, ring, rows, feature_slice = pair_send.shape
    capacity = rows // per_chunk
    _, tokens, inner = qkv.shape
    d, m = lax.axis_index("dp"), lax.axis_index("mp")
    core, x = lax.rem(m, 2), m // 2
    partner = x * 2 + 1 - core
    scale = 1.0 / math.sqrt(HD)
    mesh_id = pl.DeviceIdType.MESH

    def x_to(r):
        return lax.rem(x + r, ring)

    def target(i):
        away = peers // 2 + ((i + 1) // 2) * (1 - 2 * lax.rem(i, 2))
        return lax.rem(d + away, peers)

    def weight_copy(n):
        columns = pl.ds(n * feature_slice, feature_slice)
        return pltpu.make_async_copy(w_out.at[:, columns], wbuf.at[n], wsem.at[n])

    def residual_copy():
        columns = pl.ds(pl.multiple_of(m * feature_slice, HD), feature_slice)
        return pltpu.make_async_copy(hidden.at[:, columns], residual, rsem)

    def pair_copy(j):
        return pltpu.make_async_remote_copy(
            src_ref=pair_send.at[j], dst_ref=pair_recv.at[j],
            send_sem=pair_ssem.at[j], recv_sem=pair_rsem.at[j],
            device_id={"mp": partner}, device_id_type=mesh_id,
        )

    def x_copy(j, r):
        return pltpu.make_async_remote_copy(
            src_ref=x_send.at[j, r - 1], dst_ref=x_recv.at[j, r - 1],
            send_sem=x_ssem.at[j, r - 1], recv_sem=x_rsem.at[j, r - 1],
            device_id={"mp": x_to(r) * 2 + core}, device_id_type=mesh_id,
        )

    def own_rows():
        return out.at[pl.ds(pl.multiple_of(d * capacity, 16), capacity)]

    def row_copy(j, k):
        return pltpu.make_async_remote_copy(
            src_ref=updated.at[j, pl.ds(k * capacity, capacity)], dst_ref=own_rows(),
            send_sem=row_ssem.at[j, k], recv_sem=row_rsem.at[j, k],
            device_id={"dp": target(j * per_chunk + k)}, device_id_type=mesh_id,
        )

    def own_copy():
        return pltpu.make_async_copy(
            updated.at[chunks - 1, pl.ds(rows - capacity, capacity)], own_rows(), own_sem
        )

    for n in range(groups):
        weight_copy(n).start()
    residual_copy().start()

    barrier = pltpu.get_barrier_semaphore()
    for i in range(1, peers):
        pl.semaphore_signal(
            barrier, inc=1, device_id={"dp": lax.rem(d + i, peers)}, device_id_type=mesh_id
        )
    for r in range(1, ring):
        pl.semaphore_signal(
            barrier, inc=1, device_id={"mp": x_to(r) * 2 + core}, device_id_type=mesh_id
        )
    pl.semaphore_signal(barrier, inc=1, device_id={"mp": partner}, device_id_type=mesh_id)

    code = meta_row[1:2, :]
    hot_shape = (max(16, peers), tokens)
    hot = jnp.where(lax.broadcasted_iota(jnp.int32, hot_shape, 0) == code, 1.0, 0.0)
    below = lax.broadcasted_iota(jnp.int32, (tokens, tokens), 0)
    across = lax.broadcasted_iota(jnp.int32, (tokens, tokens), 1)
    before = jnp.where(below < across, 1.0, 0.0).astype(jnp.bfloat16)
    count = jnp.dot(hot.astype(jnp.bfloat16), before, preferred_element_type=jnp.float32)
    rank = jnp.sum(hot * count, axis=0, keepdims=True)
    slot_row[...] = jnp.where(code >= 0, code * capacity + rank.astype(jnp.int32), -1)

    pl.semaphore_wait(barrier, peers + ring - 1)
    def chosen(j):
        parts = []
        for k in range(per_chunk):
            row = lax.broadcasted_iota(jnp.int32, (capacity, tokens), 0)
            parts.append((row + target(j * per_chunk + k) * capacity) == slot_row[...])
        return jnp.concatenate(parts, axis=0) if per_chunk > 1 else parts[0]

    def as_pick(hit):
        return jnp.where(hit, 1.0, 0.0).astype(jnp.bfloat16)

    def attend(j):
        hit = chosen(j)
        places = lax.broadcasted_iota(jnp.int32, (rows, tokens), 1)
        weight = jnp.where(hit, 1.0, 0.0)
        filled = jnp.sum(weight, axis=-1, keepdims=True)
        place = jnp.sum(jnp.where(hit, places, 0).astype(jnp.float32), axis=-1, keepdims=True)
        documents = meta_row[0:1, :].astype(jnp.float32)
        document = jnp.sum(jnp.where(hit, documents, 0.0), axis=-1, keepdims=True)
        allowed = (document == documents) & (places.astype(jnp.float32) <= place)
        bias = jnp.where(allowed, 0.0, -1e30)
        queries = jnp.dot(
            weight.astype(jnp.bfloat16), qkv[0], preferred_element_type=jnp.float32
        ).astype(jnp.bfloat16)
        heads = []
        for h in range(inner // HD):
            lanes = slice(h * HD, (h + 1) * HD)
            scores = lax.dot_general(
                queries[:, lanes], qkv[1, :, lanes], (((1,), (1,)), ((), ())),
                preferred_element_type=jnp.float32,
            )
            scores = scores * scale + bias
            raised = jnp.exp(scores - jnp.max(scores, axis=-1, keepdims=True))
            total = jnp.sum(raised, axis=-1, keepdims=True)
            mixed = jnp.dot(
                raised.astype(jnp.bfloat16), qkv[2, :, lanes], preferred_element_type=jnp.float32
            )
            heads.append((mixed * (filled / total)).astype(jnp.bfloat16))
        return jnp.concatenate(heads, axis=1)

    def multiply(attended, n):
        return jnp.dot(attended, wbuf[n], preferred_element_type=jnp.float32).astype(jnp.bfloat16)

    def step(s, carry):
        @pl.when(s < chunks)
        def _():
            attended = attend(s)

            @pl.when(s == 0)
            def _():
                for n in range(groups):
                    weight_copy(n).wait()
                residual_copy().wait()

            for r in range(ring):
                pair_send[s, r] = multiply(attended, x_to(r) * 2 + 1 - core)
            pair_copy(s).start()
            for r in range(ring):
                pair_own[s, r] = multiply(attended, x_to(r) * 2 + core)
            pair_copy(s).wait_recv()
            for r in range(1, ring):
                total = pair_own[s, r].astype(jnp.float32) + pair_recv[s, r].astype(jnp.float32)
                x_send[s, r - 1] = total.astype(jnp.bfloat16)
                x_copy(s, r).start()
            kept = jnp.dot(as_pick(chosen(s)), residual[...], preferred_element_type=jnp.float32)
            acc[s] = (
                kept + pair_own[s, 0].astype(jnp.float32) + pair_recv[s, 0].astype(jnp.float32)
            )

        @pl.when(s >= LAG)
        def _():
            j = s - LAG
            total = acc[j]
            for r in range(1, ring):
                x_copy(j, r).wait_recv()
                total += x_recv[j, r - 1].astype(jnp.float32)
            updated[j] = total.astype(jnp.bfloat16)
            for k in range(per_chunk - 1):
                row_copy(j, k).start()

            @pl.when(j < chunks - 1)
            def _():
                row_copy(j, per_chunk - 1).start()

        return carry

    lax.fori_loop(0, chunks + LAG, step, 0)
    own_copy().start()

    def drain(j, carry):
        pair_copy(j).wait_send()
        for r in range(1, ring):
            x_copy(j, r).wait_send()
        for k in range(per_chunk - 1):
            row_copy(j, k).wait()

        @pl.when(j < chunks - 1)
        def _():
            row_copy(j, per_chunk - 1).wait()

        return carry

    lax.fori_loop(0, chunks, drain, 0)
    own_copy().wait()


def finish(qkv, meta, hidden, w_out, peers, groups):
    _, tokens, inner = qkv.shape
    slots = 3 * tokens // 4
    feature_slice = w_out.shape[1] // groups
    chunks = min(CHUNKS, peers)
    rows = slots // chunks
    ring = groups // 2
    dma = pltpu.SemaphoreType.DMA
    bf16 = jnp.bfloat16
    vmem = pl.BlockSpec(memory_space=VMEM)
    far = pl.BlockSpec(memory_space=ANY)
    per_chunk = peers // chunks
    return pl.pallas_call(
        functools.partial(tail_kernel, peers, groups, per_chunk),
        out_shape=jax.ShapeDtypeStruct((slots, feature_slice), bf16),
        in_specs=[vmem, vmem, far, far],
        out_specs=far,
        scratch_shapes=[
            VMEM((groups, inner, feature_slice), bf16),
            VMEM((tokens, feature_slice), bf16),
            VMEM((1, tokens), jnp.int32),
            VMEM((chunks, ring, rows, feature_slice), bf16),
            VMEM((chunks, ring, rows, feature_slice), bf16),
            VMEM((chunks, ring, rows, feature_slice), bf16),
            VMEM((chunks, ring - 1, rows, feature_slice), bf16),
            VMEM((chunks, ring - 1, rows, feature_slice), bf16),
            VMEM((chunks, rows, feature_slice), jnp.float32),
            VMEM((chunks, rows, feature_slice), bf16),
            dma((groups,)),
            dma,
            dma((chunks,)),
            dma((chunks,)),
            dma((chunks, ring - 1)),
            dma((chunks, ring - 1)),
            dma((chunks, per_chunk)),
            dma((chunks, per_chunk)),
            dma,
        ],
        compiler_params=pltpu.CompilerParams(
            collective_id=0, has_side_effects=True, vmem_limit_bytes=60 * 2**20
        ),
        name="finish",
    )(qkv, meta, hidden, w_out)


def body(hidden, exit_depth, seq_ids, dest, norm_gain, w_query, w_key, w_value, w_out):
    peers = lax.axis_size("dp")
    groups = lax.axis_size("mp")
    meta = jnp.stack([seq_ids, jnp.where(exit_depth == 3, dest, -1)])
    qkv = project(hidden, norm_gain, w_query, w_key, w_value)
    return finish(qkv, meta, hidden, w_out, peers, groups)


def solution(mesh):
    return jax.shard_map(
        body,
        mesh=mesh,
        in_specs=(
            P("dp", None),
            P("dp"),
            P("dp"),
            P("dp"),
            P(),
            P(None, "mp"),
            P(None, "mp"),
            P(None, "mp"),
            P("mp", None),
        ),
        out_specs=P("dp", "mp"),
        check_vma=False,
    )
```

profile of v0, /device:TPU:24, one launch (start us, length us, event | category | flops | bytes accessed | tf_op | source)
XLA Modules:
  0.0 114.6 jit_solution(10300850071885550348)
XLA Ops:
  0.0 0.7 compare_select_fusion
  0.7 1.3 %pad_add_fusion.meta_row = s32[2,1024]{1,0:T(2,128)} fusion(s32[1,1024]{1,0:T(1,128)S(1)} %bitcast.2, s32[1,1024]{1,0:T(1,128)} %bitcast.3), kind=kLoop, calls=%fused_computation | loop fusion | flops 2048 | bytes 16384 | tf_op jit(solution)/shard_map/stack | solution.py:368
  2.0 42.4 %qkv.1 = bf16[3,1024,768]{2,1,0:T(8,128)(2,1)} custom-call(bf16[1024,5120]{1,0:T(8,128)(2,1)} %hidden.3, bf16[5120]{0:T(1024)(128)(2,1)} %gain.1, bf16[5120,768]{1,0:T(8,128)(2,1)} %wq.1, bf16[5120,768]{1,0:T(8,128)(2,1)} %wk.1, bf16[5120,768]{1,0:T(8,128)(2,1)} %wv.1, f32[1024,128]{1,0:T(8,128)} %constant.8.clone.cosine, f32[1024,128]{1,0:T(8,128)} %constant.9.clone.sine), custom_call_target="tpu_custom_call" | custom-call | tf_op jit(solution)/shard_map/qkv/pallas_call | solution.py:105
  44.4 67.3 %finish.1 = bf16[768,1280]{1,0:T(8,128)(2,1)} custom-call(bf16[3,1024,768]{2,1,0:T(8,128)(2,1)} %qkv.1, s32[2,1024]{1,0:T(2,128)} %pad_add_fusion.meta_row, bf16[1024,5120]{1,0:T(8,128)(2,1)} %hidden.3, bf16[768,5120]{1,0:T(8,128)(2,1)} %w_out.1), custom_call_target="tpu_custom_call" | custom-call | tf_op jit(solution)/shard_map/finish/pallas_call | solution.py:332
  111.7 2.9 %copy.13 = bf16[768,1280]{1,0:T(8,128)(2,1)} copy(bf16[768,1280]{1,0:T(8,128)(2,1)} %finish.1) | data formatting | bytes 3932160
where the time goes:
time: 115 us
  Pallas kernels  110 us (96%)
  local copies, waits for them, and re-layouts  2.94 us (3%)
  other arithmetic  2 us (2%)
    pallas_call x1, Pallas kernels, finish(): pl.pallas_call(functools.partial(tail_kernel, peers, groups, per_chunk),...  67.3 us
    pallas_call x1, Pallas kernels, project(): pl.pallas_call(functools.partial(qkv_kernel, blocks, bn, rows), grid=(3 *...  42.4 us
    unnamed x1, local copies, waits for them, and re-layouts  2.94 us

commit v1 on v0

v1 whole, which is shorter than its diff:
```python
import functools
import math

import jax
import jax.numpy as jnp
import numpy as np
from jax import lax
from jax.experimental import pallas as pl
from jax.experimental.pallas import tpu as pltpu
from jax.sharding import PartitionSpec as P

HD = 128
CHUNKS = 8
LAG = 1
LOAD_ROWS = 256
ANY = pl.ANY
VMEM = pltpu.VMEM


def rope_tables(tokens):
    half = HD // 2
    frequency = 10000.0 ** (-np.arange(half, dtype=np.float64) / half)
    angle = np.arange(tokens, dtype=np.float64)[:, None] * frequency[None, :]
    cosine, sine = np.cos(angle), np.sin(angle)
    return (
        np.concatenate([cosine, cosine], axis=1).astype(np.float32),
        np.concatenate([-sine, sine], axis=1).astype(np.float32),
    )


def layer_kernel(
    peers, groups, per_chunk, bn,
    depth_row, seq_row, dest_row, gain, cosine, sine, hidden, wq, wk, wv, w_out, out,
    normed, wbuf, qkv, obuf, residual, slot_row, pair_send, pair_recv, x_send, x_recv, acc, updated,
    hsem, wsem, osem, rsem, pair_ssem, pair_rsem, x_ssem, x_rsem, row_ssem, row_rsem, own_sem,
):
    chunks, ring, rows, feature_slice = pair_send.shape
    capacity = rows // per_chunk
    _, tokens, inner = qkv.shape
    blocks = inner // bn
    loads = tokens // LOAD_ROWS
    slots = wbuf.shape[0]
    d, m = lax.axis_index("dp"), lax.axis_index("mp")
    core, x = lax.rem(m, 2), m // 2
    partner = x * 2 + 1 - core
    query_scale = math.log2(math.e) / math.sqrt(HD)
    mesh_id = pl.DeviceIdType.MESH

    def x_to(r):
        return lax.rem(x + r, ring)

    def target(i):
        away = peers // 2 + ((i + 1) // 2) * (1 - 2 * lax.rem(i, 2))
        return lax.rem(d + away, peers)

    def fetch(index, do):
        for which, w in enumerate((wk, wv, wq)):

            @pl.when(index // blocks == which)
            def _():
                column = pl.multiple_of(lax.rem(index, blocks) * bn, bn)
                to = lax.rem(index, slots)
                do(pltpu.make_async_copy(w.at[:, pl.ds(column, bn)], wbuf.at[to], wsem.at[to]))

    def hidden_copy(r):
        part = pl.ds(r * LOAD_ROWS, LOAD_ROWS)
        return pltpu.make_async_copy(hidden.at[part], normed.at[part], hsem.at[r])

    def out_weight_copy(n):
        columns = pl.ds(n * feature_slice, feature_slice)
        return pltpu.make_async_copy(w_out.at[:, columns], obuf.at[n], osem.at[n])

    def residual_copy():
        columns = pl.ds(pl.multiple_of(m * feature_slice, HD), feature_slice)
        return pltpu.make_async_copy(hidden.at[:, columns], residual, rsem)

    def pair_copy(j, r):
        return pltpu.make_async_remote_copy(
            src_ref=pair_send.at[j, r], dst_ref=pair_recv.at[j, r],
            send_sem=pair_ssem.at[j, r], recv_sem=pair_rsem.at[j, r],
            device_id={"mp": partner}, device_id_type=mesh_id,
        )

    def x_copy(j, r):
        return pltpu.make_async_remote_copy(
            src_ref=x_send.at[j, r - 1], dst_ref=x_recv.at[j, r - 1],
            send_sem=x_ssem.at[j, r - 1], recv_sem=x_rsem.at[j, r - 1],
            device_id={"mp": x_to(r) * 2 + core}, device_id_type=mesh_id,
        )

    def own_rows():
        return out.at[pl.ds(pl.multiple_of(d * capacity, 16), capacity)]

    def row_copy(j, k):
        return pltpu.make_async_remote_copy(
            src_ref=updated.at[j, pl.ds(k * capacity, capacity)], dst_ref=own_rows(),
            send_sem=row_ssem.at[j, k], recv_sem=row_rsem.at[j, k],
            device_id={"dp": target(j * per_chunk + k)}, device_id_type=mesh_id,
        )

    def own_copy():
        return pltpu.make_async_copy(
            updated.at[chunks - 1, pl.ds(rows - capacity, capacity)], own_rows(), own_sem
        )

    hidden_copy(0).start()
    fetch(0, lambda c: c.start())
    for r in range(1, loads):
        hidden_copy(r).start()
    for index in range(1, slots):
        fetch(index, lambda c: c.start())

    barrier = pltpu.get_barrier_semaphore()
    for i in range(1, peers):
        pl.semaphore_signal(
            barrier, inc=1, device_id={"dp": lax.rem(d + i, peers)}, device_id_type=mesh_id
        )
    for r in range(1, ring):
        pl.semaphore_signal(
            barrier, inc=1, device_id={"mp": x_to(r) * 2 + core}, device_id_type=mesh_id
        )
    pl.semaphore_signal(barrier, inc=1, device_id={"mp": partner}, device_id_type=mesh_id)

    code = jnp.where(depth_row[...] == 3, dest_row[...], -1)
    hot_shape = (max(16, peers), tokens)
    lanes_of = lax.broadcasted_iota(jnp.int32, hot_shape, 1)
    hot = jnp.where(lax.broadcasted_iota(jnp.int32, hot_shape, 0) == code, 1.0, 0.0)
    count, shift = hot, 1
    while shift < tokens:
        count = count + jnp.where(lanes_of >= shift, pltpu.roll(count, shift, 1), 0.0)
        shift *= 2
    rank = jnp.sum(hot * count, axis=0, keepdims=True) - 1.0
    slot_row[...] = jnp.where(code >= 0, code * capacity + rank.astype(jnp.int32), -1)

    def store(y, part, which, column, rotate, scale=None):
        for h in range(bn // HD):
            lanes = slice(h * HD, (h + 1) * HD)
            z = y[:, lanes]
            if rotate:
                z = z * cosine[part, :] + pltpu.roll(z, HD // 2, 1) * sine[part, :]
            if scale is not None:
                z = z * scale
            qkv[which, part, pl.ds(pl.multiple_of(column + h * HD, HD), HD)] = z.astype(jnp.bfloat16)

    def first(r, carry):
        hidden_copy(r).wait()
        part = pl.ds(pl.multiple_of(r * LOAD_ROWS, LOAD_ROWS), LOAD_ROWS)
        v = normed[part, :].astype(jnp.float32)
        mean_square = jnp.mean(v * v, axis=-1, keepdims=True)
        y = v * lax.rsqrt(mean_square + 1e-05) * gain[...].astype(jnp.float32)[None, :]
        normed[part, :] = y.astype(jnp.bfloat16)

        @pl.when(r == 0)
        def _():
            fetch(0, lambda c: c.wait())

        y = jnp.dot(normed[part, :], wbuf[0], preferred_element_type=jnp.float32)
        store(y, part, 0, 0, True)
        return carry

    lax.fori_loop(0, loads, first, 0)

    def project(step, carry):
        @pl.when(step - 1 + slots < 3 * blocks)
        def _():
            fetch(step - 1 + slots, lambda c: c.start())

        @pl.when(step == 1)
        def _():
            residual_copy().start()
            for n in range(groups):
                out_weight_copy(n).start()

        fetch(step, lambda c: c.wait())
        slot = lax.rem(step, slots)
        which = step // blocks
        column = lax.rem(step, blocks) * bn
        everything = slice(0, tokens)
        for rotate in (True, False):

            @pl.when((which != 1) == rotate)
            def _():
                y = jnp.dot(normed[...], wbuf[slot], preferred_element_type=jnp.float32)
                if rotate:
                    store(y, everything, which, column, True, jnp.where(which == 2, query_scale, 1.0))
                else:
                    store(y, everything, 1, column, False)

        return carry

    lax.fori_loop(1, 3 * blocks, project, 0)

    for n in range(groups):
        out_weight_copy(n).wait()
    residual_copy().wait()
    pl.semaphore_wait(barrier, peers + ring - 1)

    def chosen(j):
        parts = []
        for k in range(per_chunk):
            row = lax.broadcasted_iota(jnp.int32, (capacity, tokens), 0)
            parts.append((row + target(j * per_chunk + k) * capacity) == slot_row[...])
        return jnp.concatenate(parts, axis=0) if per_chunk > 1 else parts[0]

    def attend(j):
        hit = chosen(j)
        places = lax.broadcasted_iota(jnp.int32, (rows, tokens), 1).astype(jnp.float32)
        weight = jnp.where(hit, 1.0, 0.0)
        pick = weight.astype(jnp.bfloat16)
        filled = jnp.sum(weight, axis=-1, keepdims=True)
        place = jnp.sum(jnp.where(hit, places, 0.0), axis=-1, keepdims=True)
        documents = seq_row[...].astype(jnp.float32)
        document = jnp.sum(jnp.where(hit, documents, 0.0), axis=-1, keepdims=True)
        allowed = (document == documents) & (places <= place)
        bias = jnp.where(allowed, 0.0, -1e30)
        queries = jnp.dot(pick, qkv[2], preferred_element_type=jnp.float32).astype(jnp.bfloat16)
        heads = []
        for h in range(inner // HD):
            lanes = slice(h * HD, (h + 1) * HD)
            scores = lax.dot_general(
                queries[:, lanes], qkv[0, :, lanes], (((1,), (1,)), ((), ())),
                preferred_element_type=jnp.float32,
            )
            scores = scores + bias
            raised = jnp.exp2(scores - jnp.max(scores, axis=-1, keepdims=True))
            total = jnp.sum(raised, axis=-1, keepdims=True)
            mixed = jnp.dot(
                raised.astype(jnp.bfloat16), qkv[1, :, lanes], preferred_element_type=jnp.float32
            )
            heads.append((mixed * (filled / total)).astype(jnp.bfloat16))
        return jnp.concatenate(heads, axis=1), pick

    def multiply(attended, n):
        return jnp.dot(attended, obuf[n], preferred_element_type=jnp.float32).astype(jnp.bfloat16)

    def step(s, carry):
        @pl.when(s < chunks)
        def _():
            attended, pick = attend(s)
            order = list(range(1, ring)) + [0]
            own = {}
            for r in order:
                pair_send[s, r] = multiply(attended, x_to(r) * 2 + 1 - core)
                pair_copy(s, r).start()
                own[r] = multiply(attended, x_to(r) * 2 + core).astype(jnp.float32)
                if r == 0:
                    kept = jnp.dot(pick, residual[...], preferred_element_type=jnp.float32)
                    acc[lax.rem(s, LAG + 1)] = kept + own[0]
                else:
                    pair_copy(s, r).wait_recv()
                    total = own[r] + pair_recv[s, r].astype(jnp.float32)
                    x_send[s, r - 1] = total.astype(jnp.bfloat16)
                    x_copy(s, r).start()

        @pl.when(s >= LAG)
        def _():
            j = s - LAG
            pair_copy(j, 0).wait_recv()
            total = acc[lax.rem(j, LAG + 1)] + pair_recv[j, 0].astype(jnp.float32)
            for r in range(1, ring):
                x_copy(j, r).wait_recv()
                total += x_recv[j, r - 1].astype(jnp.float32)
            updated[j] = total.astype(jnp.bfloat16)
            for k in range(per_chunk - 1):
                row_copy(j, k).start()

            @pl.when(j < chunks - 1)
            def _():
                row_copy(j, per_chunk - 1).start()

        return carry

    lax.fori_loop(0, chunks + LAG, step, 0)
    own_copy().start()

    def drain(j, carry):
        for r in range(ring):
            pair_copy(j, r).wait_send()
        for r in range(1, ring):
            x_copy(j, r).wait_send()
        for k in range(per_chunk - 1):
            row_copy(j, k).wait()

        @pl.when(j < chunks - 1)
        def _():
            row_copy(j, per_chunk - 1).wait()

        return carry

    lax.fori_loop(0, chunks, drain, 0)
    own_copy().wait()


def body(hidden, exit_depth, seq_ids, dest, norm_gain, w_query, w_key, w_value, w_out):
    peers = lax.axis_size("dp")
    groups = lax.axis_size("mp")
    tokens, width = hidden.shape
    inner = w_query.shape[1]
    slots = 3 * tokens // 4
    feature_slice = w_out.shape[1] // groups
    chunks = min(CHUNKS, peers)
    rows = slots // chunks
    ring = groups // 2
    per_chunk = peers // chunks
    bn = 256 if inner % 256 == 0 else HD
    cosine, sine = rope_tables(tokens)
    dma = pltpu.SemaphoreType.DMA
    bf16 = jnp.bfloat16
    vmem = pl.BlockSpec(memory_space=VMEM)
    far = pl.BlockSpec(memory_space=ANY)
    line = lambda v: v.reshape(1, tokens)
    return pl.pallas_call(
        functools.partial(layer_kernel, peers, groups, per_chunk, bn),
        out_shape=jax.ShapeDtypeStruct((slots, feature_slice), bf16),
        in_specs=[vmem] * 6 + [far] * 5,
        out_specs=far,
        scratch_shapes=[
            VMEM((tokens, width), bf16),
            VMEM((3, width, bn), bf16),
            VMEM((3, tokens, inner), bf16),
            VMEM((groups, inner, feature_slice), bf16),
            VMEM((tokens, feature_slice), bf16),
            VMEM((1, tokens), jnp.int32),
            VMEM((chunks, ring, rows, feature_slice), bf16),
            VMEM((chunks, ring, rows, feature_slice), bf16),
            VMEM((chunks, ring - 1, rows, feature_slice), bf16),
            VMEM((chunks, ring - 1, rows, feature_slice), bf16),
            VMEM((LAG + 1, rows, feature_slice), jnp.float32),
            VMEM((chunks, rows, feature_slice), bf16),
            dma((tokens // LOAD_ROWS,)),
            dma((3,)),
            dma((groups,)),
            dma,
            dma((chunks, ring)),
            dma((chunks, ring)),
            dma((chunks, ring - 1)),
            dma((chunks, ring - 1)),
            dma((chunks, per_chunk)),
            dma((chunks, per_chunk)),
            dma,
        ],
        compiler_params=pltpu.CompilerParams(
            collective_id=0, has_side_effects=True, vmem_limit_bytes=60 * 2**20
        ),
        name="layer",
    )(
        line(exit_depth), line(seq_ids), line(dest), norm_gain, cosine, sine,
        hidden, w_query, w_key, w_value, w_out,
    )


def solution(mesh):
    return jax.shard_map(
        body,
        mesh=mesh,
        in_specs=(
            P("dp", None),
            P("dp"),
            P("dp"),
            P("dp"),
            P(),
            P(None, "mp"),
            P(None, "mp"),
            P(None, "mp"),
            P("mp", None),
        ),
        out_specs=P("dp", "mp"),
        check_vma=False,
    )
```

time: 115 us -> 100 us (0.87)
  Pallas kernels: 110 us -> 97.2 us
  other arithmetic: 2 us -> 0 us
    pallas_call x2 -> x1, Pallas kernels: 110 us -> 97.2 us  [body(): pl.pallas_call(functools.partial(layer_kernel, peers, groups, per_chunk,...]
    another operation x1 -> x0, other arithmetic: 1.29 us -> none  [body(): meta = jnp.stack([seq_ids, jnp.where(exit_depth == 3, dest, -1)])]
where the time goes in v1:
time: 100 us
  Pallas kernels  97.2 us (97%)
  local copies, waits for them, and re-layouts  2.94 us (3%)
    pallas_call x1, Pallas kernels, body(): pl.pallas_call(functools.partial(layer_kernel, peers, groups, per_chunk,...  97.2 us
    unnamed x1, local copies, waits for them, and re-layouts  2.94 us

profile of v1, /device:TPU:24, one launch (start us, length us, event | category | flops | bytes accessed | tf_op | source)
XLA Modules:
  0.0 100.2 jit_solution(11097486680991598943)
XLA Ops:
  0.0 97.2 %layer.1 = bf16[768,1280]{1,0:T(8,128)(2,1)} custom-call(s32[1,1024]{1,0:T(1,128)} %bitcast.3, s32[1,1024]{1,0:T(1,128)} %bitcast.4, s32[1,1024]{1,0:T(1,128)} %bitcast.5, bf16[5120]{0:T(1024)(128)(2,1)} %gain.1, f32[1024,128]{1,0:T(8,128)} %constant.4.clone.cosine, f32[1024,128]{1,0:T(8,128)} %constant.5.clone.sine, bf16[1024,5120]{1,0:T(8,128)(2,1)} %hidden.1, ...), custom_call_target="tpu_custom_call" | custom-call | tf_op jit(solution)/shard_map/layer/pallas_call | solution.py:312
  97.2 2.9 %copy.13 = bf16[768,1280]{1,0:T(8,128)(2,1)} copy(bf16[768,1280]{1,0:T(8,128)(2,1)} %layer.1) | data formatting | bytes 3932160

commit v2 on v1

v2 whole, which is shorter than its diff:
```python
import functools
import math

import jax
import jax.numpy as jnp
import numpy as np
from jax import lax
from jax.experimental import pallas as pl
from jax.experimental.pallas import tpu as pltpu
from jax.sharding import PartitionSpec as P

HD = 128
CHUNKS = 8
LAG = 1
LOAD_ROWS = 256
ANY = pl.ANY
VMEM = pltpu.VMEM


def rope_tables(tokens):
    half = HD // 2
    frequency = 10000.0 ** (-np.arange(half, dtype=np.float64) / half)
    angle = np.arange(tokens, dtype=np.float64)[:, None] * frequency[None, :]
    cosine, sine = np.cos(angle), np.sin(angle)
    return (
        np.concatenate([cosine, cosine], axis=1).astype(np.float32),
        np.concatenate([-sine, sine], axis=1).astype(np.float32),
    )


def layer_kernel(
    peers, groups, per_chunk, bn,
    depth_row, seq_row, dest_row, gain, rope, hidden, wq, wk, wv, w_out, out,
    normed, wbuf, qkv, obuf, residual, table, slot_row, pick, bias, mixed_rows,
    pair_send, pair_recv, x_send, x_recv, acc, updated,
    hsem, wsem, osem, rsem, tsem, pair_ssem, pair_rsem, x_ssem, x_rsem, row_ssem, row_rsem, own_sem,
):
    chunks, ring, halves, rows, half = pair_send.shape
    feature_slice = half * halves
    capacity = rows // per_chunk
    _, tokens, inner = qkv.shape
    blocks = inner // bn
    loads = tokens // LOAD_ROWS
    slots = wbuf.shape[0]
    d, m = lax.axis_index("dp"), lax.axis_index("mp")
    core, x = lax.rem(m, 2), m // 2
    partner = x * 2 + 1 - core
    query_scale = math.log2(math.e) / math.sqrt(HD)
    mesh_id = pl.DeviceIdType.MESH

    def x_to(r):
        return lax.rem(x + r, ring)

    def target(i):
        away = peers // 2 + ((i + 1) // 2) * (1 - 2 * lax.rem(i, 2))
        return lax.rem(d + away, peers)

    def fetch(index, do):
        for which, w in enumerate((wk, wv, wq)):

            @pl.when(index // blocks == which)
            def _():
                column = pl.multiple_of(lax.rem(index, blocks) * bn, bn)
                to = lax.rem(index, slots)
                do(pltpu.make_async_copy(w.at[:, pl.ds(column, bn)], wbuf.at[to], wsem.at[to]))

    def hidden_copy(r):
        part = pl.ds(r * LOAD_ROWS, LOAD_ROWS)
        return pltpu.make_async_copy(hidden.at[part], normed.at[part], hsem.at[r])

    def table_copy():
        return pltpu.make_async_copy(rope, table, tsem)

    def out_weight_copy(n, h):
        columns = pl.ds(n * feature_slice + h * half, half)
        return pltpu.make_async_copy(w_out.at[:, columns], obuf.at[n, h], osem.at[n, h])

    def residual_copy(h):
        columns = pl.ds(pl.multiple_of(m * feature_slice + h * half, HD), half)
        return pltpu.make_async_copy(hidden.at[:, columns], residual.at[h], rsem.at[h])

    def pair_copy(j, r, h):
        return pltpu.make_async_remote_copy(
            src_ref=pair_send.at[j, r, h], dst_ref=pair_recv.at[j, r, h],
            send_sem=pair_ssem.at[j, r, h], recv_sem=pair_rsem.at[j, r, h],
            device_id={"mp": partner}, device_id_type=mesh_id,
        )

    def x_copy(j, r, h):
        return pltpu.make_async_remote_copy(
            src_ref=x_send.at[j, r - 1, h], dst_ref=x_recv.at[j, r - 1, h],
            send_sem=x_ssem.at[j, r - 1, h], recv_sem=x_rsem.at[j, r - 1, h],
            device_id={"mp": x_to(r) * 2 + core}, device_id_type=mesh_id,
        )

    def own_rows(h):
        return out.at[pl.ds(pl.multiple_of(d * capacity, 16), capacity), pl.ds(h * half, half)]

    def row_copy(j, k, h):
        return pltpu.make_async_remote_copy(
            src_ref=updated.at[j, h, pl.ds(k * capacity, capacity)], dst_ref=own_rows(h),
            send_sem=row_ssem.at[j, k, h], recv_sem=row_rsem.at[j, k, h],
            device_id={"dp": target(j * per_chunk + k)}, device_id_type=mesh_id,
        )

    def own_copy(h):
        return pltpu.make_async_copy(
            updated.at[chunks - 1, h, pl.ds(rows - capacity, capacity)], own_rows(h), own_sem.at[h]
        )

    hidden_copy(0).start()
    fetch(0, lambda c: c.start())
    table_copy().start()
    hidden_copy(1).start()

    barrier = pltpu.get_barrier_semaphore()
    for i in range(1, peers):
        pl.semaphore_signal(
            barrier, inc=1, device_id={"dp": lax.rem(d + i, peers)}, device_id_type=mesh_id
        )
    for r in range(1, ring):
        pl.semaphore_signal(
            barrier, inc=1, device_id={"mp": x_to(r) * 2 + core}, device_id_type=mesh_id
        )
    pl.semaphore_signal(barrier, inc=1, device_id={"mp": partner}, device_id_type=mesh_id)

    code = jnp.where(depth_row[...] == 3, dest_row[...], -1)
    hot_shape = (max(16, peers), tokens)
    lanes_of = lax.broadcasted_iota(jnp.int32, hot_shape, 1)
    hot = jnp.where(lax.broadcasted_iota(jnp.int32, hot_shape, 0) == code, 1.0, 0.0)
    count, shift = hot, 1
    while shift < tokens:
        count = count + jnp.where(lanes_of >= shift, pltpu.roll(count, shift, 1), 0.0)
        shift *= 2
    rank = jnp.sum(hot * count, axis=0, keepdims=True) - 1.0
    slot_row[...] = jnp.where(code >= 0, code * capacity + rank.astype(jnp.int32), -1)

    def prepare(j):
        parts = []
        for k in range(per_chunk):
            row = lax.broadcasted_iota(jnp.int32, (capacity, tokens), 0)
            parts.append((row + target(j * per_chunk + k) * capacity) == slot_row[...])
        hit = jnp.concatenate(parts, axis=0) if per_chunk > 1 else parts[0]
        places = lax.broadcasted_iota(jnp.int32, (rows, tokens), 1).astype(jnp.float32)
        place = jnp.sum(jnp.where(hit, places, 0.0), axis=-1, keepdims=True)
        documents = seq_row[...].astype(jnp.float32)
        document = jnp.sum(jnp.where(hit, documents, 0.0), axis=-1, keepdims=True)
        allowed = (document == documents) & (places <= place)
        pick[...] = jnp.where(hit, 1.0, 0.0).astype(jnp.bfloat16)
        bias[...] = jnp.where(allowed, 0.0, -1e30)

    prepare(0)

    def store(y, part, which, column, rotate, scale=None):
        for h in range(bn // HD):
            lanes = slice(h * HD, (h + 1) * HD)
            z = y[:, lanes]
            if rotate:
                z = z * table[0, part, :] + pltpu.roll(z, HD // 2, 1) * table[1, part, :]
            if scale is not None:
                z = z * scale
            qkv[which, part, pl.ds(pl.multiple_of(column + h * HD, HD), HD)] = z.astype(jnp.bfloat16)

    def normalize(r):
        part = slice(r * LOAD_ROWS, (r + 1) * LOAD_ROWS)
        v = normed[part, :].astype(jnp.float32)
        mean_square = jnp.mean(v * v, axis=-1, keepdims=True)
        y = v * lax.rsqrt(mean_square + 1e-05) * gain[...].astype(jnp.float32)[None, :]
        normed[part, :] = y.astype(jnp.bfloat16)

    hidden_copy(0).wait()
    hidden_copy(2).start()
    normalize(0)
    fetch(0, lambda c: c.wait())
    table_copy().wait()
    for r in range(loads):
        part = slice(r * LOAD_ROWS, (r + 1) * LOAD_ROWS)
        if r + 1 < loads:
            hidden_copy(r + 1).wait()
        if r + 3 < loads:
            hidden_copy(r + 3).start()
        if 1 <= r < slots:
            fetch(r, lambda c: c.start())
        y = jnp.dot(normed[part, :], wbuf[0], preferred_element_type=jnp.float32)
        if r + 1 < loads:
            normalize(r + 1)
        store(y, part, 0, 0, True)

    def project(step, carry):
        @pl.when(step - 1 + slots < 3 * blocks)
        def _():
            fetch(step - 1 + slots, lambda c: c.start())

        @pl.when(step == 1)
        def _():
            for h in range(halves):
                residual_copy(h).start()
                for n in range(groups):
                    out_weight_copy(n, h).start()

        fetch(step, lambda c: c.wait())
        slot = lax.rem(step, slots)
        which = step // blocks
        column = lax.rem(step, blocks) * bn
        everything = slice(0, tokens)
        for rotate in (True, False):

            @pl.when((which != 1) == rotate)
            def _():
                y = jnp.dot(normed[...], wbuf[slot], preferred_element_type=jnp.float32)
                if rotate:
                    store(y, everything, which, column, True, jnp.where(which == 2, query_scale, 1.0))
                else:
                    store(y, everything, 1, column, False)

        return carry

    lax.fori_loop(1, 3 * blocks, project, 0)

    for h in range(halves):
        residual_copy(h).wait()
        for n in range(groups):
            out_weight_copy(n, h).wait()
    pl.semaphore_wait(barrier, peers + ring - 1)

    def attend():
        filled = jnp.sum(pick[...].astype(jnp.float32), axis=-1, keepdims=True)
        queries = jnp.dot(pick[...], qkv[2], preferred_element_type=jnp.float32).astype(jnp.bfloat16)
        for h in range(inner // HD):
            lanes = slice(h * HD, (h + 1) * HD)
            scores = lax.dot_general(
                queries[:, lanes], qkv[0, :, lanes], (((1,), (1,)), ((), ())),
                preferred_element_type=jnp.float32,
            )
            scores = scores + bias[...]
            raised = jnp.exp2(scores - jnp.max(scores, axis=-1, keepdims=True))
            total = jnp.sum(raised, axis=-1, keepdims=True)
            mixed = jnp.dot(
                raised.astype(jnp.bfloat16), qkv[1, :, lanes], preferred_element_type=jnp.float32
            )
            mixed_rows[:, lanes] = (mixed * (filled / total)).astype(jnp.bfloat16)

    def multiply(n, h):
        return jnp.dot(mixed_rows[...], obuf[n, h], preferred_element_type=jnp.float32).astype(
            jnp.bfloat16
        )

    def complete(j, h):
        pair_copy(j, 0, h).wait_recv()
        total = acc[lax.rem(j, LAG + 1), h] + pair_recv[j, 0, h].astype(jnp.float32)
        for r in range(1, ring):
            x_copy(j, r, h).wait_recv()
            total += x_recv[j, r - 1, h].astype(jnp.float32)
        updated[j, h] = total.astype(jnp.bfloat16)
        for k in range(per_chunk - 1):
            row_copy(j, k, h).start()

        @pl.when(j < chunks - 1)
        def _():
            row_copy(j, per_chunk - 1, h).start()

    def step(s, carry):
        @pl.when(s < chunks)
        def _():
            attend()
            for r in range(1, ring):
                for h in range(halves):
                    pair_send[s, r, h] = multiply(x_to(r) * 2 + 1 - core, h)
                    pair_copy(s, r, h).start()

        @pl.when(s >= LAG)
        def _():
            complete(s - LAG, 0)

        @pl.when(s < chunks)
        def _():
            for r in range(1, ring):
                for h in range(halves):
                    own = multiply(x_to(r) * 2 + core, h).astype(jnp.float32)
                    pair_copy(s, r, h).wait_recv()
                    total = own + pair_recv[s, r, h].astype(jnp.float32)
                    x_send[s, r - 1, h] = total.astype(jnp.bfloat16)
                    x_copy(s, r, h).start()
            for h in range(halves):
                pair_send[s, 0, h] = multiply(x * 2 + 1 - core, h)
                pair_copy(s, 0, h).start()
            for h in range(halves):
                kept = jnp.dot(pick[...], residual[h], preferred_element_type=jnp.float32)
                acc[lax.rem(s, LAG + 1), h] = kept + multiply(x * 2 + core, h).astype(jnp.float32)

        @pl.when(s >= LAG)
        def _():
            for h in range(1, halves):
                complete(s - LAG, h)

        @pl.when(s + 1 < chunks)
        def _():
            prepare(s + 1)

        return carry

    lax.fori_loop(0, chunks + LAG, step, 0)
    for h in range(halves):
        own_copy(h).start()

    def drain(j, carry):
        for h in range(halves):
            for r in range(ring):
                pair_copy(j, r, h).wait_send()
            for r in range(1, ring):
                x_copy(j, r, h).wait_send()
            for k in range(per_chunk - 1):
                row_copy(j, k, h).wait()

        @pl.when(j < chunks - 1)
        def _():
            for h in range(halves):
                row_copy(j, per_chunk - 1, h).wait()

        return carry

    lax.fori_loop(0, chunks, drain, 0)
    for h in range(halves):
        own_copy(h).wait()


def place_kernel(source, out, held, in_sem, out_sem):
    pieces, rows, _ = held.shape

    def load(i):
        return pltpu.make_async_copy(source.at[pl.ds(i * rows, rows)], held.at[i], in_sem.at[i])

    def save(i):
        return pltpu.make_async_copy(held.at[i], out.at[pl.ds(i * rows, rows)], out_sem.at[i])

    for i in range(pieces):
        load(i).start()
    for i in range(pieces):
        load(i).wait()
        save(i).start()
    for i in range(pieces):
        save(i).wait()


def body(hidden, exit_depth, seq_ids, dest, norm_gain, w_query, w_key, w_value, w_out):
    peers = lax.axis_size("dp")
    groups = lax.axis_size("mp")
    tokens, width = hidden.shape
    inner = w_query.shape[1]
    slots = 3 * tokens // 4
    feature_slice = w_out.shape[1] // groups
    chunks = min(CHUNKS, peers)
    rows = slots // chunks
    ring = groups // 2
    per_chunk = peers // chunks
    bn = 256 if inner % 256 == 0 else HD
    halves = 2 if feature_slice % (2 * HD) == 0 else 1
    half = feature_slice // halves
    rope = np.stack(rope_tables(tokens))
    dma = pltpu.SemaphoreType.DMA
    bf16 = jnp.bfloat16
    vmem = pl.BlockSpec(memory_space=VMEM)
    far = pl.BlockSpec(memory_space=ANY)
    line = lambda v: v.reshape(1, tokens)
    placed = pl.pallas_call(
        functools.partial(layer_kernel, peers, groups, per_chunk, bn),
        out_shape=jax.ShapeDtypeStruct((slots, feature_slice), bf16),
        in_specs=[vmem] * 4 + [far] * 6,
        out_specs=far,
        scratch_shapes=[
            VMEM((tokens, width), bf16),
            VMEM((3, width, bn), bf16),
            VMEM((3, tokens, inner), bf16),
            VMEM((groups, halves, inner, half), bf16),
            VMEM((halves, tokens, half), bf16),
            VMEM((2, tokens, HD), jnp.float32),
            VMEM((1, tokens), jnp.int32),
            VMEM((rows, tokens), bf16),
            VMEM((rows, tokens), jnp.float32),
            VMEM((rows, inner), bf16),
            VMEM((chunks, ring, halves, rows, half), bf16),
            VMEM((chunks, ring, halves, rows, half), bf16),
            VMEM((chunks, ring - 1, halves, rows, half), bf16),
            VMEM((chunks, ring - 1, halves, rows, half), bf16),
            VMEM((LAG + 1, halves, rows, half), jnp.float32),
            VMEM((chunks, halves, rows, half), bf16),
            dma((tokens // LOAD_ROWS,)),
            dma((3,)),
            dma((groups, halves)),
            dma((halves,)),
            dma,
            dma((chunks, ring, halves)),
            dma((chunks, ring, halves)),
            dma((chunks, ring - 1, halves)),
            dma((chunks, ring - 1, halves)),
            dma((chunks, per_chunk, halves)),
            dma((chunks, per_chunk, halves)),
            dma((halves,)),
        ],
        compiler_params=pltpu.CompilerParams(
            collective_id=0, has_side_effects=True, vmem_limit_bytes=60 * 2**20
        ),
        name="layer",
    )(
        line(exit_depth), line(seq_ids), line(dest), norm_gain, rope,
        hidden, w_query, w_key, w_value, w_out,
    )
    pieces = 4
    return pl.pallas_call(
        place_kernel,
        out_shape=jax.ShapeDtypeStruct((slots, feature_slice), bf16),
        in_specs=[far],
        out_specs=far,
        scratch_shapes=[
            VMEM((pieces, slots // pieces, feature_slice), bf16),
            dma((pieces,)),
            dma((pieces,)),
        ],
        name="place",
    )(placed)


def solution(mesh):
    return jax.shard_map(
        body,
        mesh=mesh,
        in_specs=(
            P("dp", None),
            P("dp"),
            P("dp"),
            P("dp"),
            P(),
            P(None, "mp"),
            P(None, "mp"),
            P(None, "mp"),
            P("mp", None),
        ),
        out_specs=P("dp", "mp"),
        check_vma=False,
    )
```

time: 100 us -> 98.9 us (0.989)
  local copies, waits for them, and re-layouts: 2.94 us -> 0 us
  Pallas kernels: 97.2 us -> 98.3 us
    unnamed x1 -> x0, local copies, waits for them, and re-layouts: 2.94 us -> none
    pallas_call x0 -> x1, Pallas kernels: none -> 2.36 us  [body(): pl.pallas_call(place_kernel, out_shape=jax.ShapeDtypeStruct((slots, featu...]
    pallas_call x1, Pallas kernels: 97.2 us -> 96 us  [body(): pl.pallas_call(functools.partial(layer_kernel, peers, groups, per_chunk,...]
where the time goes in v2:
time: 98.9 us; the launch traced here: 98.5 us
  Pallas kernels  98.3 us (99%)
    pallas_call x1, Pallas kernels, body(): pl.pallas_call(functools.partial(layer_kernel, peers, groups, per_chunk,...  96 us
    pallas_call x1, Pallas kernels, body(): pl.pallas_call(place_kernel, out_shape=jax.ShapeDtypeStruct((slots, featu...  2.36 us

profile of v2, /device:TPU:24, one launch (start us, length us, event | category | flops | bytes accessed | tf_op | source)
XLA Modules:
  0.0 98.5 jit_solution(285638788193004195)
XLA Ops:
  0.0 96.0 %layer.1.source = bf16[768,1280]{1,0:T(8,128)(2,1)} custom-call(s32[1,1024]{1,0:T(1,128)} %bitcast.3, s32[1,1024]{1,0:T(1,128)} %bitcast.4, s32[1,1024]{1,0:T(1,128)} %bitcast.5, bf16[5120]{0:T(1024)(128)(2,1)} %gain.1, f32[2,1024,128]{2,1,0:T(8,128)} %constant.2.clone.rope, bf16[1024,5120]{1,0:T(8,128)(2,1)} %hidden.1, bf16[5120,768]{1,0:T(8,128)(2,1)} %wq.1, ...), custom_call_target="tpu_custom_call" | custom-call | tf_op jit(solution)/shard_map/layer/pallas_call | solution.py:365
  96.0 2.4 %place.1 = bf16[768,1280]{1,0:T(8,128)(2,1)} custom-call(bf16[768,1280]{1,0:T(8,128)(2,1)} %layer.1.source), custom_call_target="tpu_custom_call" | custom-call | tf_op jit(solution)/shard_map/place/pallas_call | solution.py:409
